TPU v7x, 128 devices: a whole 4x4x4 slice. The times are simulated.
128 devices in a mesh: dp: 4 (over x), fsdp: 4 (over y), ctx: 8 (over z, core).
Axes of the slice: x: 4, y: 4, z: 4, core: 2. Of those that a mesh axis runs over, the one named last changes fastest.
Arguments:
- hidden: bfloat16 [16, 2048, 8192], P(('dp', 'fsdp'), 'ctx'), may hold values from -6 to 6
- queries: bfloat16 [16, 2048, 4096], P(('dp', 'fsdp'), 'ctx'), may hold values from -40 to 40
- rotary_keys: bfloat16 [16, 2048, 512], P(('dp', 'fsdp'), 'ctx'), may hold values from -6 to 6
- attn_cotangent: bfloat16 [16, 2048, 4096], P(('dp', 'fsdp'), 'ctx'), may hold values from -6 to 6
- value_matrix: bfloat16 [8192, 512], P(('fsdp', 'ctx')), may hold values from -0.0625 to 0.0625
- keep_index: int32 [16, 1024], P(('dp', 'fsdp')), may hold values from 0 to 2047, as said below
Outputs:
- attn: bfloat16 [16, 2048, 4096], P(('dp', 'fsdp'), 'ctx')
- grad_hidden: bfloat16 [16, 2048, 8192], P(('dp', 'fsdp'), 'ctx')
- grad_queries: bfloat16 [16, 2048, 4096], P(('dp', 'fsdp'), 'ctx')
- grad_keys: bfloat16 [16, 2048, 512], P(('dp', 'fsdp'), 'ctx')
- grad_weight: bfloat16 [8192, 512], P(('fsdp', 'ctx'))
Inputs may be any that keep to these rules, and one draw needn't show every extreme that they name: `keep_index`: each row lists 1024 distinct positions of its sequence in ascending order. For every c, the number of listed positions below c * 256 lies within 32 of c * 128, and in every row it exceeds c * 128 by exactly 32 for some c.
All inputs are finite; a program needn't handle non-finite values.
Results may differ from a plain program's by a relative error of at most 0.018.
Values may be sent and summed in bfloat16 or wider, within the bound.
No kernel may reach another device: no remote copies, remote signals or barrier semaphores. Data moves between devices by JAX's collectives and lax.ppermute only.
A program may use at most 256 MiB of HBM per device.

v0:
```python
import math

import jax
import jax.numpy as jnp
from jax import lax
from jax.experimental import pallas as pl
from jax.experimental.pallas import tpu as pltpu
from jax.sharding import PartitionSpec as P


WIDTH = 8192
HEAD = 128
HEADS = 32
GROUPS = 4
PER_GROUP = HEADS // GROUPS
KV = GROUPS * HEAD
TOK = 256
EVEN = 128
MARGIN = 32
SLOTS = EVEN + 2 * MARGIN
KEEP = 1024
PADDED = KEEP + 2 * MARGIN
SUB = 32
BLOCKS = SLOTS // SUB
LANES = SUB * PER_GROUP
SCALE = 1.0 / math.sqrt(HEAD)
LOG2E = math.log2(math.e)
BF = jnp.bfloat16
F32 = jnp.float32


CORE_SWAP = [(i, i ^ 1) for i in range(8)]
Z_UP = {k: [(i, i + 2 * k) for i in range(8 - 2 * k)] for k in (1, 2, 3)}
Z_DOWN = {k: [(t, s) for s, t in Z_UP[k]] for k in (1, 2, 3)}
RING = {k: [(i, (i + k) % 4) for i in range(4)] for k in (1, 2, 3)}
XZ_TURN = {
    k: [
        (x * 8 + 2 * z + c, ((z + k) % 4) * 8 + 2 * x + c)
        for x in range(4)
        for z in range(4)
        for c in range(2)
    ]
    for k in range(4)
}


def nt(a, b):
    return lax.dot_general(a, b, (((1,), (1,)), ((), ())), preferred_element_type=F32)


def nn(a, b):
    return jnp.dot(a, b, preferred_element_type=F32)


def owner_row(scal, rel, k):
    z, core = scal[0], scal[1]
    other = core + rel * (1 - 2 * core)
    return pl.multiple_of((jnp.maximum(z - k, 0) * 2 + other) * EVEN, EVEN)


def fill(scal, dst, own, partner):
    dst[...] = jnp.zeros_like(dst)
    for rel, part in ((0, own), (1, partner)):
        for k in range(4):
            at = owner_row(scal, rel, k)

            @pl.when(scal[0] >= k)
            def _():
                here = dst[pl.ds(at, SLOTS), :]
                dst[pl.ds(at, SLOTS), :] = here + part[k]


def windows(scal, outs, acc, scale):
    for rel in range(2):
        for k in range(4):
            at = owner_row(scal, rel, k)

            @pl.when(scal[0] >= k)
            def _():
                outs[rel][k] = (acc[pl.ds(at, SLOTS), :] * scale).astype(BF)

            @pl.when(scal[0] < k)
            def _():
                outs[rel][k] = jnp.zeros((SLOTS, HEAD), BF)


def select_kernel(scal, slot_ref, hid_ref, out_ref):
    pos = lax.broadcasted_iota(jnp.int32, (SLOTS, TOK), 1) + scal[2]
    pick = jnp.where(slot_ref[...] == pos, 1.0, 0.0).astype(BF)
    for y in range(2):
        for z in range(4):
            at = y * 2048 + z * 512
            out_ref[z, :, y * 512 : (y + 1) * 512] = nn(pick, hid_ref[0, :, at : at + 512]).astype(BF)


def select_hidden(scal, slot_col, hidden):
    return pl.pallas_call(
        select_kernel,
        grid_spec=pltpu.PrefetchScalarGridSpec(
            num_scalar_prefetch=1,
            grid=(2,),
            in_specs=[
                pl.BlockSpec((SLOTS, 1), lambda i, s: (0, 0)),
                pl.BlockSpec((1, TOK, 4096), lambda i, s: (0, 0, i)),
            ],
            out_specs=pl.BlockSpec((4, SLOTS, 1024), lambda i, s: (0, 0, i)),
        ),
        out_shape=jax.ShapeDtypeStruct((4, SLOTS, 2048), BF),
        name="select_hidden",
    )(scal, slot_col, hidden)


def values_kernel(hid_ref, w_ref, out_ref, acc):
    @pl.when(pl.program_id(0) == 0)
    def _():
        acc[...] = jnp.zeros_like(acc)

    total = acc[...]
    for z in range(4):
        total = total + nn(hid_ref[z], w_ref[z * 512 : (z + 1) * 512, :])
    acc[...] = total
    out_ref[...] = total.astype(BF)


def values_call(pieces, weight):
    return pl.pallas_call(
        values_kernel,
        grid=(4,),
        in_specs=[
            pl.BlockSpec((4, SLOTS, 512), lambda i: (0, 0, i)),
            pl.BlockSpec((2048, KV), lambda i: (i, 0)),
        ],
        out_specs=pl.BlockSpec((SLOTS, KV), lambda i: (0, 0)),
        out_shape=jax.ShapeDtypeStruct((SLOTS, KV), BF),
        scratch_shapes=[pltpu.VMEM((SLOTS, KV), F32)],
        name="values",
    )(pieces, weight)


def weight_kernel(scal, h0, h1, h2, h3, g0, g1, g2, g3, own_ref, other_ref, acc):
    total = None
    for h, g in ((h0, g0), (h1, g1), (h2, g2), (h3, g3)):
        term = lax.dot_general(h[0], g[...], (((0,), (0,)), ((), ())), preferred_element_type=F32)
        total = term if total is None else total + term
    acc[...] = total
    own_ref[0] = acc[pl.ds(pl.multiple_of(scal[1] * 256, 256), 256), :].astype(BF)
    other_ref[0] = acc[pl.ds(pl.multiple_of((1 - scal[1]) * 256, 256), 256), :].astype(BF)


def weight_call(scal, hid, grad):
    cols = [pl.BlockSpec((1, SLOTS, 512), lambda i, s, k=k: ((s[3] - k) & 3, 0, i)) for k in range(4)]
    rows = pl.BlockSpec((SLOTS, KV), lambda i, s: (0, 0))
    out = pl.BlockSpec((1, 256, KV), lambda i, s: ((i - s[5]) & 3, 0, 0))
    return pl.pallas_call(
        weight_kernel,
        grid_spec=pltpu.PrefetchScalarGridSpec(
            num_scalar_prefetch=1,
            grid=(4,),
            in_specs=cols + [rows] * 4,
            out_specs=[out, out],
            scratch_shapes=[pltpu.VMEM((512, KV), F32)],
        ),
        out_shape=[jax.ShapeDtypeStruct((4, 256, KV), BF)] * 2,
        name="weight_terms",
    )(scal, hid, hid, hid, hid, *grad)


def hidden_grad_kernel(gv_ref, w_ref, out_ref):
    out_ref[0] = nt(gv_ref[...], w_ref[...]).astype(BF)


def hidden_grad(gv_pos, weight):
    return pl.pallas_call(
        hidden_grad_kernel,
        grid=(4,),
        in_specs=[pl.BlockSpec((TOK, KV), lambda i: (0, 0)), pl.BlockSpec((2048, KV), lambda i: (i, 0))],
        out_specs=pl.BlockSpec((1, TOK, 2048), lambda i: (0, 0, i)),
        out_shape=jax.ShapeDtypeStruct((1, TOK, WIDTH), BF),
        name="hidden_grad",
    )(gv_pos, weight)


def probs_kernel(scal, slot_ref, q_ref, cot_ref, ko_ref, kp_ref, p_ref, qs_ref, cs_ref, k_ref, dv0_ref, dv1_ref, acc):
    start, base = scal[2], scal[4]
    pos = lax.broadcasted_iota(jnp.int32, (SLOTS, TOK), 1) + start
    pick = jnp.where(slot_ref[...] == pos, 1.0, 0.0).astype(BF)
    for src, dst in ((q_ref, qs_ref), (cot_ref, cs_ref)):
        rows = nn(pick, src[0]).astype(BF)
        for b in range(BLOCKS):
            for h in range(PER_GROUP):
                dst[0, b * LANES + h * SUB : b * LANES + (h + 1) * SUB, :] = rows[
                    b * SUB : (b + 1) * SUB, h * HEAD : (h + 1) * HEAD
                ]
    fill(scal, k_ref, ko_ref, kp_ref)
    acc[...] = jnp.zeros_like(acc)
    keys = k_ref[MARGIN : MARGIN + KEEP, :]
    key_id = lax.broadcasted_iota(jnp.int32, (KEEP, LANES), 0)
    lane_id = lax.broadcasted_iota(jnp.int32, (1, LANES), 1) & (SUB - 1)

    def scores(b):
        return nt(keys, qs_ref[0, b * LANES : (b + 1) * LANES, :])

    ahead = scores(0)
    for b in range(BLOCKS):
        at = b * LANES
        s = ahead
        if b + 1 < BLOCKS:
            ahead = scores(b + 1)
        s = jnp.where(key_id <= lane_id + (base + b * SUB), s, -1e30)
        top = jnp.max(s, axis=0, keepdims=True)
        e = jnp.exp2((s - top) * (SCALE * LOG2E))
        total = jnp.sum(e, axis=0, keepdims=True)
        p = (e * (1.0 / total)).astype(BF)
        p_ref[0, b] = p
        acc[MARGIN : MARGIN + KEEP, :] += nn(p, cs_ref[0, at : at + LANES, :])
    windows(scal, (dv0_ref, dv1_ref), acc, 1.0)


def probs_call(scal, slot_col, queries, cot, k_own, k_partner):
    rows = pl.BlockSpec((1, TOK, 1024), lambda g, s: (0, 0, g))
    piece = pl.BlockSpec((4, SLOTS, HEAD), lambda g, s: (0, 0, g))
    stack = pl.BlockSpec((1, BLOCKS * LANES, HEAD), lambda g, s: (g, 0, 0))
    return pl.pallas_call(
        probs_kernel,
        grid_spec=pltpu.PrefetchScalarGridSpec(
            num_scalar_prefetch=1,
            grid=(GROUPS,),
            in_specs=[pl.BlockSpec((SLOTS, 1), lambda g, s: (0, 0)), rows, rows, piece, piece],
            out_specs=[
                pl.BlockSpec((1, BLOCKS, KEEP, LANES), lambda g, s: (g, 0, 0, 0)),
                stack,
                stack,
                pl.BlockSpec((PADDED, HEAD), lambda g, s: (0, g)),
                piece,
                piece,
            ],
            scratch_shapes=[pltpu.VMEM((PADDED, HEAD), F32)],
        ),
        out_shape=[
            jax.ShapeDtypeStruct((GROUPS, BLOCKS, KEEP, LANES), BF),
            jax.ShapeDtypeStruct((GROUPS, BLOCKS * LANES, HEAD), BF),
            jax.ShapeDtypeStruct((GROUPS, BLOCKS * LANES, HEAD), BF),
            jax.ShapeDtypeStruct((PADDED, KV), BF),
            jax.ShapeDtypeStruct((4, SLOTS, KV), BF),
            jax.ShapeDtypeStruct((4, SLOTS, KV), BF),
        ],
        name="probs_and_value_grad",
    )(scal, slot_col, queries, cot, k_own, k_partner)


def grads_kernel(scal, slot_ref, p_ref, qs_ref, cs_ref, k_ref, vo_ref, vp_ref, *rest):
    at_ref, gq_ref, dk0_ref, dk1_ref, acc, v_scr, o_scr, g_scr = rest[-8:]
    start = scal[2]
    fill(scal, v_scr, vo_ref, vp_ref)
    acc[...] = jnp.zeros_like(acc)
    keys = k_ref[MARGIN : MARGIN + KEEP, :]
    vals = v_scr[MARGIN : MARGIN + KEEP, :]
    keys_t = keys.T
    vals_t = vals.T
    for b in range(BLOCKS):
        at = b * LANES
        p = p_ref[0, b]
        cot = cs_ref[0, at : at + LANES, :]
        out_t = nn(vals_t, p).astype(BF).astype(F32)
        cot_t = cot.astype(F32).T
        row_dot = jnp.sum(out_t * cot_t, axis=0, keepdims=True)
        ds = (p.astype(F32) * (nt(vals, cot) - row_dot)).astype(BF)
        gq_t = nn(keys_t, ds) * SCALE
        acc[MARGIN : MARGIN + KEEP, :] += nn(ds, qs_ref[0, at : at + LANES, :])
        out = out_t.T.astype(BF)
        gq = gq_t.T.astype(BF)
        for h in range(PER_GROUP):
            o_scr[b * SUB : (b + 1) * SUB, h * HEAD : (h + 1) * HEAD] = out[h * SUB : (h + 1) * SUB, :]
            g_scr[b * SUB : (b + 1) * SUB, h * HEAD : (h + 1) * HEAD] = gq[h * SUB : (h + 1) * SUB, :]
    pos = lax.broadcasted_iota(jnp.int32, (TOK, SLOTS), 0) + start
    place = jnp.where(slot_ref[...] == pos, 1.0, 0.0).astype(BF)
    at_ref[0] = nn(place, o_scr[...]).astype(BF)
    gq_ref[0] = nn(place, g_scr[...]).astype(BF)
    windows(scal, (dk0_ref, dk1_ref), acc, SCALE)


def grads_call(scal, slot_row, probs, qs, cs, keys, v_own, v_partner):
    piece = pl.BlockSpec((4, SLOTS, HEAD), lambda g, s: (0, 0, g))
    stack = pl.BlockSpec((1, BLOCKS * LANES, HEAD), lambda g, s: (g, 0, 0))
    rows = pl.BlockSpec((1, TOK, 1024), lambda g, s: (0, 0, g))
    whole = jax.ShapeDtypeStruct((1, TOK, HEADS * HEAD), BF)
    terms = jax.ShapeDtypeStruct((4, SLOTS, KV), BF)
    return pl.pallas_call(
        grads_kernel,
        grid_spec=pltpu.PrefetchScalarGridSpec(
            num_scalar_prefetch=1,
            grid=(GROUPS,),
            in_specs=[
                pl.BlockSpec((1, SLOTS), lambda g, s: (0, 0)),
                pl.BlockSpec((1, BLOCKS, KEEP, LANES), lambda g, s: (g, 0, 0, 0)),
                stack,
                stack,
                pl.BlockSpec((PADDED, HEAD), lambda g, s: (0, g)),
                piece,
                piece,
            ],
            out_specs=[rows, rows, piece, piece],
            scratch_shapes=[
                pltpu.VMEM((PADDED, HEAD), F32),
                pltpu.VMEM((PADDED, HEAD), BF),
                pltpu.VMEM((SLOTS, PER_GROUP * HEAD), BF),
                pltpu.VMEM((SLOTS, PER_GROUP * HEAD), BF),
            ],
        ),
        out_shape=[whole, whole, terms, terms],
        name="attention_grads",
    )(scal, slot_row, probs, qs, cs, keys, v_own, v_partner)


def to_later(piece, beside=()):
    got = [lax.ppermute(piece, "ctx", Z_UP[k]) for k in (2, 1, 3)]
    own = jnp.stack([piece, got[1], got[0], got[2]])
    if beside:
        own, *beside = lax.optimization_barrier((own, *beside))
    partner = lax.ppermute(own, "ctx", CORE_SWAP)
    return own, partner, beside


def to_owner(same, other, after=None):
    swapped = lax.ppermute(other, "ctx", CORE_SWAP)
    both = [(same[k].astype(F32) + swapped[k].astype(F32)).astype(BF) for k in range(4)]
    got = [both[0]] + [lax.ppermute(both[k], "ctx", Z_DOWN[k]) for k in (2, 1, 3)]
    if after is not None:
        got = lax.optimization_barrier((after, *got))[1:]
    return sum(g.astype(F32) for g in got).astype(BF), both[0]


def local(hidden, queries, rotary_keys, attn_cotangent, value_matrix, keep_index):
    ctx = lax.axis_index("ctx")
    z, core = ctx // 2, ctx % 2
    start = ctx * TOK
    base = ctx * EVEN - MARGIN
    scal = jnp.stack([z, core, start, lax.axis_index("dp"), base, lax.axis_index("fsdp")]).astype(jnp.int32)
    fence = jnp.full((MARGIN,), -1, jnp.int32)
    padded = jnp.concatenate([fence, keep_index[0], fence])
    slot = lax.dynamic_slice(padded, (ctx * EVEN,), (SLOTS,))
    slot_col, slot_row = slot[:, None], slot[None, :]
    here = start + jnp.arange(TOK, dtype=jnp.int32)
    pick = (slot_col == here[None, :]).astype(BF)
    place = (slot_row == here[:, None]).astype(BF)

    weight = lax.all_gather(value_matrix, ("fsdp", "ctx"), axis=0, tiled=True)

    k_rows = nn(pick, rotary_keys[0]).astype(BF)
    pieces = select_hidden(scal, slot_col, hidden)
    k_own, k_partner, (pieces,) = to_later(k_rows, (pieces,))
    hid = lax.all_to_all(pieces, "dp", 0, 0, tiled=True)

    probs, qs, cs, keys, dv_same, dv_other = probs_call(
        scal, slot_col, queries, attn_cotangent, k_own, k_partner
    )

    v_rows = values_call(pieces, weight)
    grad_values, _ = to_owner(dv_same, dv_other, v_rows)
    v_own, v_partner, _ = to_later(v_rows)

    gv = [grad_values] + [lax.ppermute(grad_values, "dp", RING[k]) for k in (1, 2, 3)]
    dw_same, dw_other = weight_call(scal, hid, gv)
    swapped = lax.ppermute(dw_other, "ctx", CORE_SWAP)
    both = [dw_same[k].astype(F32) + swapped[k].astype(F32) for k in range(4)]
    total = both[0]
    both = [b.astype(BF) for b in both]
    got = [lax.ppermute(both[k], "fsdp", RING[k]) for k in (2, 1, 3)]

    attn, gq, dk_same, dk_other = grads_call(scal, slot_row, probs, qs, cs, keys, v_own, v_partner)
    gk_rows, dk_first = to_owner(dk_same, dk_other)

    got = lax.optimization_barrier((dk_first, *got))[1:]
    total = sum((g.astype(F32) for g in got), total).astype(BF)
    got = [lax.ppermute(total, ("dp", "ctx"), XZ_TURN[k]) for k in range(4)]
    grad_weight = sum(g.astype(F32) for g in got).astype(BF)

    gv_late, dk_other = lax.optimization_barrier((grad_values, dk_other))
    grad_hidden = hidden_grad(nn(place, gv_late).astype(BF), weight)
    grad_keys = nn(place, gk_rows).astype(BF)
    return (attn, grad_hidden, gq, grad_keys[None], grad_weight)


def solution(mesh):
    rows = P(("dp", "fsdp"), "ctx", None)
    weight = P(("fsdp", "ctx"), None)

    return jax.shard_map(
        local,
        mesh=mesh,
        in_specs=(rows, rows, rows, rows, weight, P(("dp", "fsdp"), None)),
        out_specs=(rows, rows, rows, rows, weight),
        check_vma=False,
    )
```

profile of v0, /device:TPU:18, one launch (start us, length us, event | category | flops | bytes accessed | tf_op | source)
XLA Modules:
  0.0 191.4 jit_solution(17873000412309082710)
XLA Ops:
  9.0 3.8 %collective-permute-start = (bf16[192,512]{1,0:T(8,128)(2,1)S(1)}, bf16[192,512]{1,0:T(8,128)(2,1)S(1)}, u32[]{:S(2)}, u32[]{:S(2)}) collective-permute-start(bf16[192,512]{1,0:T(8,128)(2,1)S(1)} %convolution_convert_fusion.2), channel_id=1, source_target_pairs={{0,2},{1,3},{2,4},{3,5},{4,6},{5,7},{8,10},{9,11},{10,12},{11,13},... | collective-permute-start | bytes 589832 | tf_op jit(solution)/shard_map/ppermute | solution.py:316
  12.9 5.5 %collective-permute-start.1 = (bf16[192,512]{1,0:T(8,128)(2,1)S(1)}, bf16[192,512]{1,0:T(8,128)(2,1)S(1)}, u32[]{:S(2)}, u32[]{:S(2)}) collective-permute-start(bf16[192,512]{1,0:T(8,128)(2,1)S(1)} %convolution_convert_fusion.2), channel_id=1, source_target_pairs={{0,4},{1,5},{2,6},{3,7},{8,12},{9,13},{10,14},{11,15},{16,20},{17,... | collective-permute-start | bytes 589832 | tf_op jit(solution)/shard_map/ppermute | solution.py:316
  18.4 1.3 collective-permute-start.2
  21.1 4.8 %select_hidden.1.hid_ref = bf16[4,192,2048]{2,1,0:T(8,128)(2,1)} custom-call(s32[6]{0:T(128)} %stack.57.scal, s32[192,1]{1,0:T(8,128)} %copy.12.slot_ref, bf16[1,256,8192]{2,1,0:T(8,128)(2,1)} %hid_ref.1), custom_call_target="tpu_custom_call" | custom-call | tf_op jit(solution)/shard_map/select_hidden/pallas_call | solution.py:97
  27.4 4.8 %all-to-all-start = ((bf16[4,192,2048]{2,1,0:T(8,128)(2,1)}), bf16[4,192,2048]{2,1,0:T(8,128)(2,1)S(1)}, u32[]{:S(2)}, u32[]{:S(2)}) async-start(bf16[4,192,2048]{2,1,0:T(8,128)(2,1)} %select_hidden.1.hid_ref), calls=%async_computation | async-start | bytes 6291456 | tf_op jit(solution)/shard_map/all_to_all | solution.py:352
  32.2 19.9 %probs_and_value_grad.1 = (bf16[4,6,1024,256]{3,2,1,0:T(8,128)(2,1)}, bf16[4,1536,128]{2,1,0:T(8,128)(2,1)}, bf16[4,1536,128]{2,1,0:T(8,128)(2,1)}, bf16[1088,51...) custom-call(s32[6]{0:T(128)} %stack.57.scal, s32[192,1]{1,0:T(8,128)} %copy.12.slot_ref, ...), custom_call_target="tpu_custom_call" | custom-call | tf_op jit(solution)/shard_map/probs_and_value_grad/pallas_call | solution.py:223
  52.1 2.7 %collective-permute-done.8 = bf16[4,192,512]{2,1,0:T(8,128)(2,1)S(1)} collective-permute-done((bf16[4,192,512]{2,1,0:T(8,128)(2,1)}, bf16[4,192,512]{2,1,0:T(8,128)(2,1)S(1)}, u32[]{:S(2)}, u32[]{:S(2)}) %collective-permute-start.8) | collective-permute-done | bytes 786464 | tf_op jit(solution)/shard_map/ppermute | solution.py:325
  54.9 2.2 %fusion.13 = (bf16[192,512]{1,0:T(8,128)(2,1)}, bf16[192,512]{1,0:T(8,128)(2,1)}, bf16[192,512]{1,0:T(8,128)(2,1)S(1)}, bf16[192,512]{1,0:T(8,128)(2,1)}) fusion(bf16[4,192,512]{2,1,0:T(8,128)(2,1)S(1)} %collective-permute-done.8, bf16[4,192,512]{2,1,0:T(8,128)(2,1)} %get-tuple-element.34), kind=kLoop, calls=%fused_computation.33 | loop fusion | flops 1572864 | bytes 2359296 | tf_op jit(solution)/shard_map/convert_element_type | solution.py:326
  61.0 4.4 %all-gather.2.cloned.1.call-done.w_ref = bf16[8192,512]{1,0:T(8,128)(2,1)} async-done(((bf16[256,512]{1,0:T(8,128)(2,1)}), bf16[8192,512]{1,0:T(8,128)(2,1)}) %all-gather.2.cloned.1.call-update) | async-done | bytes 8388624 | tf_op jit(solution)/shard_map/all_gather | solution.py:347
  65.3 6.6 %values.1 = bf16[192,512]{1,0:T(8,128)(2,1)} custom-call(bf16[4,192,2048]{2,1,0:T(8,128)(2,1)} %select_hidden.1.hid_ref, bf16[8192,512]{1,0:T(8,128)(2,1)} %all-gather.2.cloned.1.call-done.w_ref), custom_call_target="tpu_custom_call" | custom-call | tf_op jit(solution)/shard_map/values/pallas_call | solution.py:126
  72.0 5.4 %collective-permute-start.4 = (bf16[192,512]{1,0:T(8,128)(2,1)}, bf16[192,512]{1,0:T(8,128)(2,1)S(1)}, u32[]{:S(2)}, u32[]{:S(2)}) collective-permute-start(bf16[192,512]{1,0:T(8,128)(2,1)} %values.1), channel_id=1, source_target_pairs={{0,2},{1,3},{2,4},{3,5},{4,6},{5,7},{8,10},{9,11},{10,12},{11,13},... | collective-permute-start | bytes 589832 | tf_op jit(solution)/shard_map/ppermute | solution.py:316
  77.3 2.2 %collective-permute-start.5 = (bf16[192,512]{1,0:T(8,128)(2,1)}, bf16[192,512]{1,0:T(8,128)(2,1)S(1)}, u32[]{:S(2)}, u32[]{:S(2)}) collective-permute-start(bf16[192,512]{1,0:T(8,128)(2,1)} %values.1), channel_id=1, source_target_pairs={{0,4},{1,5},{2,6},{3,7},{8,12},{9,13},{10,14},{11,15},{16,20},{17,... | collective-permute-start | bytes 589832 | tf_op jit(solution)/shard_map/ppermute | solution.py:316
  79.6 1.3 collective-permute-start.6
  80.9 2.0 %collective-permute-done.4 = bf16[192,512]{1,0:T(8,128)(2,1)S(1)} collective-permute-done((bf16[192,512]{1,0:T(8,128)(2,1)}, bf16[192,512]{1,0:T(8,128)(2,1)S(1)}, u32[]{:S(2)}, u32[]{:S(2)}) %collective-permute-start.4) | collective-permute-done | bytes 196640 | tf_op jit(solution)/shard_map/ppermute | solution.py:316
  82.9 3.5 %collective-permute-done.5 = bf16[192,512]{1,0:T(8,128)(2,1)S(1)} collective-permute-done((bf16[192,512]{1,0:T(8,128)(2,1)}, bf16[192,512]{1,0:T(8,128)(2,1)S(1)}, u32[]{:S(2)}, u32[]{:S(2)}) %collective-permute-start.5) | collective-permute-done | bytes 196640 | tf_op jit(solution)/shard_map/ppermute | solution.py:316
  87.4 1.9 pad_maximum_fusion.1.vo_ref
  89.3 1.3 add_convert_fusion.9.g0
  90.7 1.5 collective-permute-start.16
  92.2 1.7 collective-permute-start.17
  93.9 1.5 collective-permute-start.18
  95.5 3.2 %collective-permute-done.16.g1 = bf16[192,512]{1,0:T(8,128)(2,1)} collective-permute-done((bf16[192,512]{1,0:T(8,128)(2,1)S(1)}, bf16[192,512]{1,0:T(8,128)(2,1)}, u32[]{:S(2)}, u32[]{:S(2)}) %collective-permute-start.16) | collective-permute-done | bytes 196640 | tf_op jit(solution)/shard_map/ppermute | solution.py:362
  98.6 3.0 %collective-permute-done.17.g2 = bf16[192,512]{1,0:T(8,128)(2,1)} collective-permute-done((bf16[192,512]{1,0:T(8,128)(2,1)S(1)}, bf16[192,512]{1,0:T(8,128)(2,1)}, u32[]{:S(2)}, u32[]{:S(2)}) %collective-permute-start.17) | collective-permute-done | bytes 196640 | tf_op jit(solution)/shard_map/ppermute | solution.py:362
  101.7 3.3 %collective-permute-done.18.g3 = bf16[192,512]{1,0:T(8,128)(2,1)} collective-permute-done((bf16[192,512]{1,0:T(8,128)(2,1)S(1)}, bf16[192,512]{1,0:T(8,128)(2,1)}, u32[]{:S(2)}, u32[]{:S(2)}) %collective-permute-start.18) | collective-permute-done | bytes 196640 | tf_op jit(solution)/shard_map/ppermute | solution.py:362
  105.0 6.9 %weight_terms.1 = (bf16[4,256,512]{2,1,0:T(8,128)(2,1)}, bf16[4,256,512]{2,1,0:T(8,128)(2,1)}) custom-call(s32[6]{0:T(128)} %stack.57.scal, bf16[4,192,2048]{2,1,0:T(8,128)(2,1)} %copy-done.2, bf16[4,192,2048]{2,1,0:T(8,128)(2,1)} %copy-done.2, bf16[4,192,2048]{2,1,0:T(8,128)(2,1)} %copy-done.2, bf16[4,192,2048]{2,1,0:T(8,128)(2,1)} %copy-done.2, ...), custom_call_target="tpu_custom_call" | custom-call | tf_op jit(solution)/shard_map/weight_terms/pallas_call | solution.py:154
  111.9 19.2 %attention_grads.1 = (bf16[1,256,4096]{2,1,0:T(8,128)(2,1)}, bf16[1,256,4096]{2,1,0:T(8,128)(2,1)}, bf16[4,192,512]{2,1,0:T(8,128)(2,1)}, bf16[4,192,512]{2,1,0:T(8,128)(2,1)}) custom-call(s32[6]{0:T(128)} %stack.57.scal, s32[1,192]{1,0:T(1,128)} %bitcast.62, bf16[4,6,1024,256]{3,2,1,0:T(8,128)(2,1)} %get-tuple-element.28.p_ref, ...), custom_call_target="tpu_custom_call" | custom-call | tf_op jit(solution)/shard_map/attention_grads/pallas_call | solution.py:288
  132.8 2.0 %collective-permute-start.21 = (bf16[256,512]{1,0:T(8,128)(2,1)S(1)}, bf16[256,512]{1,0:T(8,128)(2,1)S(1)}, u32[]{:S(2)}, u32[]{:S(2)}) collective-permute-start(bf16[256,512]{1,0:T(8,128)(2,1)S(1)} %get-tuple-element.50), channel_id=1, source_target_pairs={{0,8},{8,16},{16,24},{24,0},{1,9},{9,17},{17,25},{25,1},{2,10},{10... | collective-permute-start | bytes 786440 | tf_op jit(solution)/shard_map/ppermute | solution.py:368
  135.1 7.7 %collective-permute-done.20 = bf16[256,512]{1,0:T(8,128)(2,1)S(1)} collective-permute-done((bf16[256,512]{1,0:T(8,128)(2,1)S(1)}, bf16[256,512]{1,0:T(8,128)(2,1)S(1)}, u32[]{:S(2)}, u32[]{:S(2)}) %collective-permute-start.20) | collective-permute-done | bytes 262176 | tf_op jit(solution)/shard_map/ppermute | solution.py:368
  142.8 3.7 %collective-permute-done.21 = bf16[256,512]{1,0:T(8,128)(2,1)S(1)} collective-permute-done((bf16[256,512]{1,0:T(8,128)(2,1)S(1)}, bf16[256,512]{1,0:T(8,128)(2,1)S(1)}, u32[]{:S(2)}, u32[]{:S(2)}) %collective-permute-start.21) | collective-permute-done | bytes 262176 | tf_op jit(solution)/shard_map/ppermute | solution.py:368
  149.5 4.3 %collective-permute-start.23 = (bf16[256,512]{1,0:T(8,128)(2,1)S(1)}, bf16[256,512]{1,0:T(8,128)(2,1)S(1)}, u32[]{:S(2)}, u32[]{:S(2)}) collective-permute-start(bf16[256,512]{1,0:T(8,128)(2,1)S(1)} %fusion.3), channel_id=1, source_target_pairs={{0,0},{1,1},{2,32},{3,33},{4,64},{5,65},{6,96},{7,97},{32,2},{33,3... | collective-permute-start | bytes 786440 | tf_op jit(solution)/shard_map/ppermute | solution.py:375
  153.9 3.3 %collective-permute-start.25 = (bf16[256,512]{1,0:T(8,128)(2,1)S(1)}, bf16[256,512]{1,0:T(8,128)(2,1)S(1)}, u32[]{:S(2)}, u32[]{:S(2)}) collective-permute-start(bf16[256,512]{1,0:T(8,128)(2,1)S(1)} %fusion.3), channel_id=1, source_target_pairs={{0,64},{1,65},{2,96},{3,97},{4,0},{5,1},{6,32},{7,33},{32,66},{33,... | collective-permute-start | bytes 786440 | tf_op jit(solution)/shard_map/ppermute | solution.py:375
  157.2 16.0 %collective-permute-start.26 = (bf16[256,512]{1,0:T(8,128)(2,1)S(1)}, bf16[256,512]{1,0:T(8,128)(2,1)S(1)}, u32[]{:S(2)}, u32[]{:S(2)}) collective-permute-start(bf16[256,512]{1,0:T(8,128)(2,1)S(1)} %fusion.3), channel_id=1, source_target_pairs={{0,96},{1,97},{2,0},{3,1},{4,32},{5,33},{6,64},{7,65},{32,98},{33,... | collective-permute-start | bytes 786440 | tf_op jit(solution)/shard_map/ppermute | solution.py:375
  175.5 7.2 %hidden_grad.1 = bf16[1,256,8192]{2,1,0:T(8,128)(2,1)} custom-call(bf16[256,512]{1,0:T(8,128)(2,1)} %convolution_convert_fusion.1.gv_ref, bf16[8192,512]{1,0:T(8,128)(2,1)} %all-gather.2.cloned.1.call-done.w_ref), custom_call_target="tpu_custom_call" | custom-call | tf_op jit(solution)/shard_map/hidden_grad/pallas_call | solution.py:173
  (68 shorter events, 18.6 us)
Async XLA Ops:
  7.2 58.2 %all-gather.2.cloned.1.call-start = ((), (), s32[]{:S(2)}) async-start(), calls=%async_computation.1 | async-start | bytes 8650752 | tf_op jit(solution)/shard_map/all_gather | solution.py:347
  9.0 17.0 %collective-permute-start = (bf16[192,512]{1,0:T(8,128)(2,1)S(1)}, bf16[192,512]{1,0:T(8,128)(2,1)S(1)}, u32[]{:S(2)}, u32[]{:S(2)}) collective-permute-start(bf16[192,512]{1,0:T(8,128)(2,1)S(1)} %convolution_convert_fusion.2), channel_id=1, source_target_pairs={{0,2},{1,3},{2,4},{3,5},{4,6},{5,7},{8,10},{9,11},{10,12},{11,13},... | collective-permute-start | bytes 589832 | tf_op jit(solution)/shard_map/ppermute | solution.py:316
  12.9 13.1 %collective-permute-start.1 = (bf16[192,512]{1,0:T(8,128)(2,1)S(1)}, bf16[192,512]{1,0:T(8,128)(2,1)S(1)}, u32[]{:S(2)}, u32[]{:S(2)}) collective-permute-start(bf16[192,512]{1,0:T(8,128)(2,1)S(1)} %convolution_convert_fusion.2), channel_id=1, source_target_pairs={{0,4},{1,5},{2,6},{3,7},{8,12},{9,13},{10,14},{11,15},{16,20},{17,... | collective-permute-start | bytes 589832 | tf_op jit(solution)/shard_map/ppermute | solution.py:316
  18.4 8.0 %collective-permute-start.2 = (bf16[192,512]{1,0:T(8,128)(2,1)S(1)}, bf16[192,512]{1,0:T(8,128)(2,1)S(1)}, u32[]{:S(2)}, u32[]{:S(2)}) collective-permute-start(bf16[192,512]{1,0:T(8,128)(2,1)S(1)} %convolution_convert_fusion.2), channel_id=1, source_target_pairs={{0,6},{1,7},{8,14},{9,15},{16,22},{17,23},{24,30},{25,31},{32,38},... | collective-permute-start | bytes 589832 | tf_op jit(solution)/shard_map/ppermute | solution.py:316
  27.3 4.9 %collective-permute-start.3 = (bf16[4,192,512]{2,1,0:T(8,128)(2,1)}, bf16[4,192,512]{2,1,0:T(8,128)(2,1)}, u32[]{:S(2)}, u32[]{:S(2)}) collective-permute-start(bf16[4,192,512]{2,1,0:T(8,128)(2,1)} %pad_maximum_fusion.ko_ref), channel_id=1, source_target_pairs={{0,1},{1,0},{2,3},{3,2},{4,5},{5,4},{6,7},{7,6},{8,9},{9,8},{10,11... | collective-permute-start | bytes 2359304 | tf_op jit(solution)/shard_map/ppermute | solution.py:320
  27.4 68.1 %all-to-all-start = ((bf16[4,192,2048]{2,1,0:T(8,128)(2,1)}), bf16[4,192,2048]{2,1,0:T(8,128)(2,1)S(1)}, u32[]{:S(2)}, u32[]{:S(2)}) async-start(bf16[4,192,2048]{2,1,0:T(8,128)(2,1)} %select_hidden.1.hid_ref), calls=%async_computation | async-start | bytes 6291456 | tf_op jit(solution)/shard_map/all_to_all | solution.py:352
  52.1 2.8 %collective-permute-start.8 = (bf16[4,192,512]{2,1,0:T(8,128)(2,1)}, bf16[4,192,512]{2,1,0:T(8,128)(2,1)S(1)}, u32[]{:S(2)}, u32[]{:S(2)}) collective-permute-start(bf16[4,192,512]{2,1,0:T(8,128)(2,1)} %get-tuple-element.35), channel_id=1, source_target_pairs={{0,1},{1,0},{2,3},{3,2},{4,5},{5,4},{6,7},{7,6},{8,9},{9,8},{10,11... | collective-permute-start | bytes 2359304 | tf_op jit(solution)/shard_map/ppermute | solution.py:325
  57.1 22.5 %collective-permute-start.10 = (bf16[192,512]{1,0:T(8,128)(2,1)}, bf16[192,512]{1,0:T(8,128)(2,1)}, u32[]{:S(2)}, u32[]{:S(2)}) collective-permute-start(bf16[192,512]{1,0:T(8,128)(2,1)} %get-tuple-element.57), channel_id=1, source_target_pairs={{2,0},{3,1},{4,2},{5,3},{6,4},{7,5},{10,8},{11,9},{12,10},{13,11},... | collective-permute-start | bytes 589832 | tf_op jit(solution)/shard_map/ppermute | solution.py:327
  58.4 22.5 %collective-permute-start.11 = (bf16[192,512]{1,0:T(8,128)(2,1)}, bf16[192,512]{1,0:T(8,128)(2,1)}, u32[]{:S(2)}, u32[]{:S(2)}) collective-permute-start(bf16[192,512]{1,0:T(8,128)(2,1)} %get-tuple-element.56), channel_id=1, source_target_pairs={{6,0},{7,1},{14,8},{15,9},{22,16},{23,17},{30,24},{31,25},{38,32},... | collective-permute-start | bytes 589832 | tf_op jit(solution)/shard_map/ppermute | solution.py:327
  59.7 21.2 %collective-permute-start.9 = (bf16[192,512]{1,0:T(8,128)(2,1)S(1)}, bf16[192,512]{1,0:T(8,128)(2,1)}, u32[]{:S(2)}, u32[]{:S(2)}) collective-permute-start(bf16[192,512]{1,0:T(8,128)(2,1)S(1)} %get-tuple-element.58), channel_id=1, source_target_pairs={{4,0},{5,1},{6,2},{7,3},{12,8},{13,9},{14,10},{15,11},{20,16},{21,... | collective-permute-start | bytes 589832 | tf_op jit(solution)/shard_map/ppermute | solution.py:327
  72.0 10.9 %collective-permute-start.4 = (bf16[192,512]{1,0:T(8,128)(2,1)}, bf16[192,512]{1,0:T(8,128)(2,1)S(1)}, u32[]{:S(2)}, u32[]{:S(2)}) collective-permute-start(bf16[192,512]{1,0:T(8,128)(2,1)} %values.1), channel_id=1, source_target_pairs={{0,2},{1,3},{2,4},{3,5},{4,6},{5,7},{8,10},{9,11},{10,12},{11,13},... | collective-permute-start | bytes 589832 | tf_op jit(solution)/shard_map/ppermute | solution.py:316
  77.3 9.1 %collective-permute-start.5 = (bf16[192,512]{1,0:T(8,128)(2,1)}, bf16[192,512]{1,0:T(8,128)(2,1)S(1)}, u32[]{:S(2)}, u32[]{:S(2)}) collective-permute-start(bf16[192,512]{1,0:T(8,128)(2,1)} %values.1), channel_id=1, source_target_pairs={{0,4},{1,5},{2,6},{3,7},{8,12},{9,13},{10,14},{11,15},{16,20},{17,... | collective-permute-start | bytes 589832 | tf_op jit(solution)/shard_map/ppermute | solution.py:316
  79.6 7.9 %collective-permute-start.6 = (bf16[192,512]{1,0:T(8,128)(2,1)}, bf16[192,512]{1,0:T(8,128)(2,1)S(1)}, u32[]{:S(2)}, u32[]{:S(2)}) collective-permute-start(bf16[192,512]{1,0:T(8,128)(2,1)} %values.1), channel_id=1, source_target_pairs={{0,6},{1,7},{8,14},{9,15},{16,22},{17,23},{24,30},{25,31},{32,38},... | collective-permute-start | bytes 589832 | tf_op jit(solution)/shard_map/ppermute | solution.py:316
  89.3 22.6 %collective-permute-start.7 = (bf16[4,192,512]{2,1,0:T(8,128)(2,1)}, bf16[4,192,512]{2,1,0:T(8,128)(2,1)}, u32[]{:S(2)}, u32[]{:S(2)}) collective-permute-start(bf16[4,192,512]{2,1,0:T(8,128)(2,1)} %pad_maximum_fusion.1.vo_ref), channel_id=1, source_target_pairs={{0,1},{1,0},{2,3},{3,2},{4,5},{5,4},{6,7},{7,6},{8,9},{9,8},{10,11... | collective-permute-start | bytes 2359304 | tf_op jit(solution)/shard_map/ppermute | solution.py:320
  90.7 8.0 %collective-permute-start.16 = (bf16[192,512]{1,0:T(8,128)(2,1)S(1)}, bf16[192,512]{1,0:T(8,128)(2,1)}, u32[]{:S(2)}, u32[]{:S(2)}) collective-permute-start(bf16[192,512]{1,0:T(8,128)(2,1)S(1)} %add_convert_fusion.9.g0), channel_id=1, source_target_pairs={{0,32},{32,64},{64,96},{96,0},{1,33},{33,65},{65,97},{97,1},{2,34}... | collective-permute-start | bytes 589832 | tf_op jit(solution)/shard_map/ppermute | solution.py:362
  92.2 9.4 %collective-permute-start.17 = (bf16[192,512]{1,0:T(8,128)(2,1)S(1)}, bf16[192,512]{1,0:T(8,128)(2,1)}, u32[]{:S(2)}, u32[]{:S(2)}) collective-permute-start(bf16[192,512]{1,0:T(8,128)(2,1)S(1)} %add_convert_fusion.9.g0), channel_id=1, source_target_pairs={{0,64},{32,96},{64,0},{96,32},{1,65},{33,97},{65,1},{97,33},{2,66}... | collective-permute-start | bytes 589832 | tf_op jit(solution)/shard_map/ppermute | solution.py:362
  93.9 11.0 %collective-permute-start.18 = (bf16[192,512]{1,0:T(8,128)(2,1)S(1)}, bf16[192,512]{1,0:T(8,128)(2,1)}, u32[]{:S(2)}, u32[]{:S(2)}) collective-permute-start(bf16[192,512]{1,0:T(8,128)(2,1)S(1)} %add_convert_fusion.9.g0), channel_id=1, source_target_pairs={{0,96},{32,0},{64,32},{96,64},{1,97},{33,1},{65,33},{97,65},{2,98}... | collective-permute-start | bytes 589832 | tf_op jit(solution)/shard_map/ppermute | solution.py:362
  111.9 19.8 %collective-permute-start.19 = (bf16[4,256,512]{2,1,0:T(8,128)(2,1)}, bf16[4,256,512]{2,1,0:T(8,128)(2,1)S(1)}, u32[]{:S(2)}, u32[]{:S(2)}) collective-permute-start(bf16[4,256,512]{2,1,0:T(8,128)(2,1)} %get-tuple-element.45), channel_id=1, source_target_pairs={{0,1},{1,0},{2,3},{3,2},{4,5},{5,4},{6,7},{7,6},{8,9},{9,8},{10,11... | collective-permute-start | bytes 3145736 | tf_op jit(solution)/shard_map/ppermute | solution.py:364
  111.9 19.8 %copy-start.5 = (bf16[4,256,512]{2,1,0:T(8,128)(2,1)S(1)}, bf16[4,256,512]{2,1,0:T(8,128)(2,1)}, u32[]{:S(2)}) copy-start(bf16[4,256,512]{2,1,0:T(8,128)(2,1)} %get-tuple-element.44) | copy-start | bytes 3145732
  131.2 3.7 %collective-permute-start.12 = (bf16[4,192,512]{2,1,0:T(8,128)(2,1)}, bf16[4,192,512]{2,1,0:T(8,128)(2,1)S(1)}, u32[]{:S(2)}, u32[]{:S(2)}) collective-permute-start(bf16[4,192,512]{2,1,0:T(8,128)(2,1)} %get-tuple-element.40), channel_id=1, source_target_pairs={{0,1},{1,0},{2,3},{3,2},{4,5},{5,4},{6,7},{7,6},{8,9},{9,8},{10,11... | collective-permute-start | bytes 2359304 | tf_op jit(solution)/shard_map/ppermute | solution.py:325
  131.9 42.5 %copy-start.4 = (bf16[192,512]{1,0:T(8,128)(2,1)S(1)}, bf16[192,512]{1,0:T(8,128)(2,1)}, u32[]{:S(2)}) copy-start(bf16[192,512]{1,0:T(8,128)(2,1)} %copy-done.3) | copy-start | bytes 589828
  132.0 42.5 %copy-start.8 = (s32[192]{0:T(256)S(1)}, s32[192]{0:T(256)}, u32[]{:S(2)}) copy-start(s32[192]{0:T(256)} %copy-done.7) | copy-start | bytes 2308
  132.0 10.8 %collective-permute-start.20 = (bf16[256,512]{1,0:T(8,128)(2,1)S(1)}, bf16[256,512]{1,0:T(8,128)(2,1)S(1)}, u32[]{:S(2)}, u32[]{:S(2)}) collective-permute-start(bf16[256,512]{1,0:T(8,128)(2,1)S(1)} %get-tuple-element.51), channel_id=1, source_target_pairs={{0,16},{8,24},{16,0},{24,8},{1,17},{9,25},{17,1},{25,9},{2,18},{10... | collective-permute-start | bytes 786440 | tf_op jit(solution)/shard_map/ppermute | solution.py:368
  132.8 13.7 %collective-permute-start.21 = (bf16[256,512]{1,0:T(8,128)(2,1)S(1)}, bf16[256,512]{1,0:T(8,128)(2,1)S(1)}, u32[]{:S(2)}, u32[]{:S(2)}) collective-permute-start(bf16[256,512]{1,0:T(8,128)(2,1)S(1)} %get-tuple-element.50), channel_id=1, source_target_pairs={{0,8},{8,16},{16,24},{24,0},{1,9},{9,17},{17,25},{25,1},{2,10},{10... | collective-permute-start | bytes 786440 | tf_op jit(solution)/shard_map/ppermute | solution.py:368
  134.8 11.9 %collective-permute-start.22 = (bf16[256,512]{1,0:T(8,128)(2,1)S(1)}, bf16[256,512]{1,0:T(8,128)(2,1)S(1)}, u32[]{:S(2)}, u32[]{:S(2)}) collective-permute-start(bf16[256,512]{1,0:T(8,128)(2,1)S(1)} %get-tuple-element.49), channel_id=1, source_target_pairs={{0,24},{8,0},{16,8},{24,16},{1,25},{9,1},{17,9},{25,17},{2,26},{10... | collective-permute-start | bytes 786440 | tf_op jit(solution)/shard_map/ppermute | solution.py:368
  146.7 10.5 %collective-permute-start.13 = (bf16[192,512]{1,0:T(8,128)(2,1)S(1)}, bf16[192,512]{1,0:T(8,128)(2,1)S(1)}, u32[]{:S(2)}, u32[]{:S(2)}) collective-permute-start(bf16[192,512]{1,0:T(8,128)(2,1)S(1)} %get-tuple-element.55), channel_id=1, source_target_pairs={{4,0},{5,1},{6,2},{7,3},{12,8},{13,9},{14,10},{15,11},{20,16},{21,... | collective-permute-start | bytes 589832 | tf_op jit(solution)/shard_map/ppermute | solution.py:327
  148.0 25.2 %collective-permute-start.14 = (bf16[192,512]{1,0:T(8,128)(2,1)S(1)}, bf16[192,512]{1,0:T(8,128)(2,1)S(1)}, u32[]{:S(2)}, u32[]{:S(2)}) collective-permute-start(bf16[192,512]{1,0:T(8,128)(2,1)S(1)} %get-tuple-element.54), channel_id=1, source_target_pairs={{2,0},{3,1},{4,2},{5,3},{6,4},{7,5},{10,8},{11,9},{12,10},{13,11},... | collective-permute-start | bytes 589832 | tf_op jit(solution)/shard_map/ppermute | solution.py:327
  149.5 34.2 %collective-permute-start.23 = (bf16[256,512]{1,0:T(8,128)(2,1)S(1)}, bf16[256,512]{1,0:T(8,128)(2,1)S(1)}, u32[]{:S(2)}, u32[]{:S(2)}) collective-permute-start(bf16[256,512]{1,0:T(8,128)(2,1)S(1)} %fusion.3), channel_id=1, source_target_pairs={{0,0},{1,1},{2,32},{3,33},{4,64},{5,65},{6,96},{7,97},{32,2},{33,3... | collective-permute-start | bytes 786440 | tf_op jit(solution)/shard_map/ppermute | solution.py:375
  153.8 29.9 %collective-permute-start.24 = (bf16[256,512]{1,0:T(8,128)(2,1)S(1)}, bf16[256,512]{1,0:T(8,128)(2,1)S(1)}, u32[]{:S(2)}, u32[]{:S(2)}) collective-permute-start(bf16[256,512]{1,0:T(8,128)(2,1)S(1)} %fusion.3), channel_id=1, source_target_pairs={{0,32},{1,33},{2,64},{3,65},{4,96},{5,97},{6,0},{7,1},{32,34},{33,... | collective-permute-start | bytes 786440 | tf_op jit(solution)/shard_map/ppermute | solution.py:375
  153.9 29.8 %collective-permute-start.25 = (bf16[256,512]{1,0:T(8,128)(2,1)S(1)}, bf16[256,512]{1,0:T(8,128)(2,1)S(1)}, u32[]{:S(2)}, u32[]{:S(2)}) collective-permute-start(bf16[256,512]{1,0:T(8,128)(2,1)S(1)} %fusion.3), channel_id=1, source_target_pairs={{0,64},{1,65},{2,96},{3,97},{4,0},{5,1},{6,32},{7,33},{32,66},{33,... | collective-permute-start | bytes 786440 | tf_op jit(solution)/shard_map/ppermute | solution.py:375
  157.2 26.5 %collective-permute-start.26 = (bf16[256,512]{1,0:T(8,128)(2,1)S(1)}, bf16[256,512]{1,0:T(8,128)(2,1)S(1)}, u32[]{:S(2)}, u32[]{:S(2)}) collective-permute-start(bf16[256,512]{1,0:T(8,128)(2,1)S(1)} %fusion.3), channel_id=1, source_target_pairs={{0,96},{1,97},{2,0},{3,1},{4,32},{5,33},{6,64},{7,65},{32,98},{33,... | collective-permute-start | bytes 786440 | tf_op jit(solution)/shard_map/ppermute | solution.py:375
  173.2 9.5 %collective-permute-start.15 = (bf16[192,512]{1,0:T(8,128)(2,1)S(1)}, bf16[192,512]{1,0:T(8,128)(2,1)S(1)}, u32[]{:S(2)}, u32[]{:S(2)}) collective-permute-start(bf16[192,512]{1,0:T(8,128)(2,1)S(1)} %get-tuple-element.53), channel_id=1, source_target_pairs={{6,0},{7,1},{14,8},{15,9},{22,16},{23,17},{30,24},{31,25},{38,32},... | collective-permute-start | bytes 589832 | tf_op jit(solution)/shard_map/ppermute | solution.py:327
  (6 other events, 55.4 us)
Sparse Core Ops, SparseCore 0:
  10.3 55.0 all-gather.1
where the time goes:
time: 192 us; the launch traced here: 191 us
  Pallas kernels  64.7 us (34%)
  starting transfers between devices  64.1 us (33%)
  waiting for transfers between devices  35.8 us (19%)
  between operations  14.4 us (8%)
  other arithmetic  7.84 us (4%)
  local copies, waits for them, and re-layouts  2.33 us (1%)
  matrix products  2.23 us (1%)
    ppermute x4, starting transfers between devices, local(): got = [lax.ppermute(total, ('dp', 'ctx'), XZ_TURN[k]) for k in range(4)]  23.7 us
    pallas_call x1, Pallas kernels, probs_call(): pl.pallas_call(probs_kernel, grid_spec=pltpu.PrefetchScalarGridSpec(num_s...  19.9 us
    ppermute x6, starting transfers between devices, to_later(): got = [lax.ppermute(piece, 'ctx', Z_UP[k]) for k in (2, 1, 3)]  19.5 us
    pallas_call x1, Pallas kernels, grads_call(): pl.pallas_call(grads_kernel, grid_spec=pltpu.PrefetchScalarGridSpec(num_s...  19.2 us
    ppermute x3, waiting for transfers between devices, local(): got = [lax.ppermute(both[k], 'fsdp', RING[k]) for k in (2, 1, 3)]  11.6 us
    ppermute x3, waiting for transfers between devices, local(): lax.ppermute(grad_values, 'dp', RING[k])  9.49 us
    ppermute x6, starting transfers between devices, to_owner(): lax.ppermute(both[k], 'ctx', Z_DOWN[k])  7.72 us
    pallas_call x1, Pallas kernels, hidden_grad(): pl.pallas_call(hidden_grad_kernel, grid=(4,), in_specs=[pl.BlockSpec((TOK...  7.21 us
  transfers between devices with their start and end apart: 29, of which 12 were waited for; matrix products, arithmetic and copies ran while one was open for 6% of the time, Pallas kernels for 34%

commit v1 on v0

--- a/solution.py
+++ b/solution.py
@@ -248,10 +248,12 @@
     )(scal, slot_col, queries, cot, k_own, k_partner)
 
 
-def grads_kernel(scal, slot_ref, p_ref, qs_ref, cs_ref, k_ref, vo_ref, vp_ref, *rest):
+def grads_kernel(scal, slot_ref, p_ref, qs_ref, cs_ref, k_ref, v_ref, *rest):
     at_ref, gq_ref, dk0_ref, dk1_ref, acc, v_scr, o_scr, g_scr = rest[-8:]
     start = scal[2]
-    fill(scal, v_scr, vo_ref, vp_ref)
+    v_scr[...] = jnp.zeros_like(v_scr)
+    for i in range(8):
+        v_scr[i * EVEN : i * EVEN + SLOTS, :] += v_ref[i]
     acc[...] = jnp.zeros_like(acc)
     keys = k_ref[MARGIN : MARGIN + KEEP, :]
     vals = v_scr[MARGIN : MARGIN + KEEP, :]
@@ -279,7 +281,7 @@
     windows(scal, (dk0_ref, dk1_ref), acc, SCALE)
 
 
-def grads_call(scal, slot_row, probs, qs, cs, keys, v_own, v_partner):
+def grads_call(scal, slot_row, probs, qs, cs, keys, every_v):
     piece = pl.BlockSpec((4, SLOTS, HEAD), lambda g, s: (0, 0, g))
     stack = pl.BlockSpec((1, BLOCKS * LANES, HEAD), lambda g, s: (g, 0, 0))
     rows = pl.BlockSpec((1, TOK, 1024), lambda g, s: (0, 0, g))
@@ -296,8 +298,7 @@
                 stack,
                 stack,
                 pl.BlockSpec((PADDED, HEAD), lambda g, s: (0, g)),
-                piece,
-                piece,
+                pl.BlockSpec((8, SLOTS, HEAD), lambda g, s: (0, 0, g)),
             ],
             out_specs=[rows, rows, piece, piece],
             scratch_shapes=[
@@ -309,7 +310,7 @@
         ),
         out_shape=[whole, whole, terms, terms],
         name="attention_grads",
-    )(scal, slot_row, probs, qs, cs, keys, v_own, v_partner)
+    )(scal, slot_row, probs, qs, cs, keys, every_v)
 
 
 def to_later(piece, beside=()):
@@ -357,7 +358,7 @@
 
     v_rows = values_call(pieces, weight)
     grad_values, _ = to_owner(dv_same, dv_other, v_rows)
-    v_own, v_partner, _ = to_later(v_rows)
+    every_v = lax.all_gather(v_rows, "ctx", axis=0, tiled=False)
 
     gv = [grad_values] + [lax.ppermute(grad_values, "dp", RING[k]) for k in (1, 2, 3)]
     dw_same, dw_other = weight_call(scal, hid, gv)
@@ -367,7 +368,7 @@
     both = [b.astype(BF) for b in both]
     got = [lax.ppermute(both[k], "fsdp", RING[k]) for k in (2, 1, 3)]
 
-    attn, gq, dk_same, dk_other = grads_call(scal, slot_row, probs, qs, cs, keys, v_own, v_partner)
+    attn, gq, dk_same, dk_other = grads_call(scal, slot_row, probs, qs, cs, keys, every_v)
     gk_rows, dk_first = to_owner(dk_same, dk_other)
 
     got = lax.optimization_barrier((dk_first, *got))[1:]
@@ -375,8 +376,7 @@
     got = [lax.ppermute(total, ("dp", "ctx"), XZ_TURN[k]) for k in range(4)]
     grad_weight = sum(g.astype(F32) for g in got).astype(BF)
 
-    gv_late, dk_other = lax.optimization_barrier((grad_values, dk_other))
-    grad_hidden = hidden_grad(nn(place, gv_late).astype(BF), weight)
+    grad_hidden = hidden_grad(nn(place, grad_values).astype(BF), weight)
     grad_keys = nn(place, gk_rows).astype(BF)
     return (attn, grad_hidden, gq, grad_keys[None], grad_weight)
 

time: 192 us -> 209 us (1.089)
  the two profiles are of different devices: /device:TPU:18 before, /device:TPU:32 now
where the time goes in v1:
time: 209 us; the launch traced here: 208 us
  waiting for transfers between devices  77.5 us (37%)
  Pallas kernels  64.7 us (31%)
  starting transfers between devices  42.6 us (20%)
  between operations  14.3 us (7%)
  other arithmetic  3.95 us (2%)
  local copies, waits for them, and re-layouts  2.26 us (1%)
  matrix products  2.23 us (1%)
    all_gather x1, waiting for transfers between devices, local(): weight = lax.all_gather(value_matrix, ('fsdp', 'ctx'), axis=0, tiled=True)  37.5 us
    pallas_call x1, Pallas kernels, probs_call(): pl.pallas_call(probs_kernel, grid_spec=pltpu.PrefetchScalarGridSpec(num_s...  19.9 us
    pallas_call x1, Pallas kernels, grads_call(): pl.pallas_call(grads_kernel, grid_spec=pltpu.PrefetchScalarGridSpec(num_s...  19.2 us
    ppermute x6, waiting for transfers between devices, to_owner(): lax.ppermute(both[k], 'ctx', Z_DOWN[k])  19.2 us
    ppermute x4, starting transfers between devices, local(): got = [lax.ppermute(total, ('dp', 'ctx'), XZ_TURN[k]) for k in range(4)]  10.8 us
    ppermute x3, waiting for transfers between devices, local(): got = [lax.ppermute(both[k], 'fsdp', RING[k]) for k in (2, 1, 3)]  10.1 us
    ppermute x6, starting transfers between devices, to_owner(): lax.ppermute(both[k], 'ctx', Z_DOWN[k])  8.95 us
    ppermute x3, waiting for transfers between devices, local(): lax.ppermute(grad_values, 'dp', RING[k])  7.68 us
  transfers between devices with their start and end apart: 26, of which 9 were waited for; matrix products, arithmetic and copies ran while one was open for 4% of the time, Pallas kernels for 31%

profile of v1, /device:TPU:32, one launch (start us, length us, event | category | flops | bytes accessed | tf_op | source)
XLA Modules:
  0.0 207.5 jit_solution(12350842628606260181)
XLA Ops:
  9.0 3.8 %collective-permute-start = (bf16[192,512]{1,0:T(8,128)(2,1)S(1)}, bf16[192,512]{1,0:T(8,128)(2,1)S(1)}, u32[]{:S(2)}, u32[]{:S(2)}) collective-permute-start(bf16[192,512]{1,0:T(8,128)(2,1)S(1)} %convolution_convert_fusion.2), channel_id=1, source_target_pairs={{0,2},{1,3},{2,4},{3,5},{4,6},{5,7},{8,10},{9,11},{10,12},{11,13},... | collective-permute-start | bytes 589832 | tf_op jit(solution)/shard_map/ppermute | solution.py:317
  12.9 2.4 %collective-permute-start.1 = (bf16[192,512]{1,0:T(8,128)(2,1)S(1)}, bf16[192,512]{1,0:T(8,128)(2,1)S(1)}, u32[]{:S(2)}, u32[]{:S(2)}) collective-permute-start(bf16[192,512]{1,0:T(8,128)(2,1)S(1)} %convolution_convert_fusion.2), channel_id=1, source_target_pairs={{0,4},{1,5},{2,6},{3,7},{8,12},{9,13},{10,14},{11,15},{16,20},{17,... | collective-permute-start | bytes 589832 | tf_op jit(solution)/shard_map/ppermute | solution.py:317
  17.3 4.7 %select_hidden.1.hid_ref = bf16[4,192,2048]{2,1,0:T(8,128)(2,1)} custom-call(s32[6]{0:T(128)} %stack.42.scal, s32[192,1]{1,0:T(8,128)} %copy.12.slot_ref, bf16[1,256,8192]{2,1,0:T(8,128)(2,1)} %hid_ref.1), custom_call_target="tpu_custom_call" | custom-call | tf_op jit(solution)/shard_map/select_hidden/pallas_call | solution.py:97
  23.0 4.3 %all-to-all-start = ((bf16[4,192,2048]{2,1,0:T(8,128)(2,1)}), bf16[4,192,2048]{2,1,0:T(8,128)(2,1)S(1)}, u32[]{:S(2)}, u32[]{:S(2)}) async-start(bf16[4,192,2048]{2,1,0:T(8,128)(2,1)} %select_hidden.1.hid_ref), calls=%async_computation | async-start | bytes 6291456 | tf_op jit(solution)/shard_map/all_to_all | solution.py:353
  27.3 37.5 %all-gather.4.cloned.1.call-done.w_ref = bf16[8192,512]{1,0:T(8,128)(2,1)} async-done(((bf16[256,512]{1,0:T(8,128)(2,1)}), bf16[8192,512]{1,0:T(8,128)(2,1)}) %all-gather.4.cloned.1.call-update) | async-done | bytes 8388624 | tf_op jit(solution)/shard_map/all_gather | solution.py:348
  64.8 6.6 %values.1 = bf16[192,512]{1,0:T(8,128)(2,1)} custom-call(bf16[4,192,2048]{2,1,0:T(8,128)(2,1)} %select_hidden.1.hid_ref, bf16[8192,512]{1,0:T(8,128)(2,1)} %all-gather.4.cloned.1.call-done.w_ref), custom_call_target="tpu_custom_call" | custom-call | tf_op jit(solution)/shard_map/values/pallas_call | solution.py:126
  71.5 19.9 %probs_and_value_grad.1 = (bf16[4,6,1024,256]{3,2,1,0:T(8,128)(2,1)}, bf16[4,1536,128]{2,1,0:T(8,128)(2,1)}, bf16[4,1536,128]{2,1,0:T(8,128)(2,1)}, bf16[1088,51...) custom-call(s32[6]{0:T(128)} %stack.42.scal, s32[192,1]{1,0:T(8,128)} %copy.12.slot_ref, ...), custom_call_target="tpu_custom_call" | custom-call | tf_op jit(solution)/shard_map/probs_and_value_grad/pallas_call | solution.py:223
  91.7 2.3 %collective-permute-done.4 = bf16[4,192,512]{2,1,0:T(8,128)(2,1)S(1)} collective-permute-done((bf16[4,192,512]{2,1,0:T(8,128)(2,1)}, bf16[4,192,512]{2,1,0:T(8,128)(2,1)S(1)}, u32[]{:S(2)}, u32[]{:S(2)}) %collective-permute-start.4) | collective-permute-done | bytes 786464 | tf_op jit(solution)/shard_map/ppermute | solution.py:326
  94.0 1.4 fusion.13
  95.4 1.3 collective-permute-start.5
  96.7 2.7 %collective-permute-start.6 = (bf16[192,512]{1,0:T(8,128)(2,1)S(1)}, bf16[192,512]{1,0:T(8,128)(2,1)S(1)}, u32[]{:S(2)}, u32[]{:S(2)}) collective-permute-start(bf16[192,512]{1,0:T(8,128)(2,1)S(1)} %get-tuple-element.55), channel_id=1, source_target_pairs={{2,0},{3,1},{4,2},{5,3},{6,4},{7,5},{10,8},{11,9},{12,10},{13,11},... | collective-permute-start | bytes 589832 | tf_op jit(solution)/shard_map/ppermute | solution.py:328
  100.1 6.5 %collective-permute-done.5 = bf16[192,512]{1,0:T(8,128)(2,1)S(1)} collective-permute-done((bf16[192,512]{1,0:T(8,128)(2,1)S(1)}, bf16[192,512]{1,0:T(8,128)(2,1)S(1)}, u32[]{:S(2)}, u32[]{:S(2)}) %collective-permute-start.5) | collective-permute-done | bytes 196640 | tf_op jit(solution)/shard_map/ppermute | solution.py:328
  106.7 3.6 %collective-permute-done.6 = bf16[192,512]{1,0:T(8,128)(2,1)S(1)} collective-permute-done((bf16[192,512]{1,0:T(8,128)(2,1)S(1)}, bf16[192,512]{1,0:T(8,128)(2,1)S(1)}, u32[]{:S(2)}, u32[]{:S(2)}) %collective-permute-start.6) | collective-permute-done | bytes 196640 | tf_op jit(solution)/shard_map/ppermute | solution.py:328
  110.4 1.5 collective-permute-start.12
  111.9 2.7 %collective-permute-start.13 = (bf16[192,512]{1,0:T(8,128)(2,1)S(1)}, bf16[192,512]{1,0:T(8,128)(2,1)}, u32[]{:S(2)}, u32[]{:S(2)}) collective-permute-start(bf16[192,512]{1,0:T(8,128)(2,1)S(1)} %add_convert_fusion.9.g0), channel_id=1, source_target_pairs={{0,64},{32,96},{64,0},{96,32},{1,65},{33,97},{65,1},{97,33},{2,66}... | collective-permute-start | bytes 589832 | tf_op jit(solution)/shard_map/ppermute | solution.py:363
  114.6 1.5 collective-permute-start.14
  116.0 2.5 %collective-permute-done.12.g1 = bf16[192,512]{1,0:T(8,128)(2,1)} collective-permute-done((bf16[192,512]{1,0:T(8,128)(2,1)S(1)}, bf16[192,512]{1,0:T(8,128)(2,1)}, u32[]{:S(2)}, u32[]{:S(2)}) %collective-permute-start.12) | collective-permute-done | bytes 196640 | tf_op jit(solution)/shard_map/ppermute | solution.py:363
  118.6 5.1 %collective-permute-done.13.g2 = bf16[192,512]{1,0:T(8,128)(2,1)} collective-permute-done((bf16[192,512]{1,0:T(8,128)(2,1)S(1)}, bf16[192,512]{1,0:T(8,128)(2,1)}, u32[]{:S(2)}, u32[]{:S(2)}) %collective-permute-start.13) | collective-permute-done | bytes 196640 | tf_op jit(solution)/shard_map/ppermute | solution.py:363
  123.7 6.9 %weight_terms.1 = (bf16[4,256,512]{2,1,0:T(8,128)(2,1)}, bf16[4,256,512]{2,1,0:T(8,128)(2,1)}) custom-call(s32[6]{0:T(128)} %stack.42.scal, bf16[4,192,2048]{2,1,0:T(8,128)(2,1)} %copy-done.2, bf16[4,192,2048]{2,1,0:T(8,128)(2,1)} %copy-done.2, bf16[4,192,2048]{2,1,0:T(8,128)(2,1)} %copy-done.2, bf16[4,192,2048]{2,1,0:T(8,128)(2,1)} %copy-done.2, ...), custom_call_target="tpu_custom_call" | custom-call | tf_op jit(solution)/shard_map/weight_terms/pallas_call | solution.py:154
  130.7 19.2 %attention_grads.1 = (bf16[1,256,4096]{2,1,0:T(8,128)(2,1)}, bf16[1,256,4096]{2,1,0:T(8,128)(2,1)}, bf16[4,192,512]{2,1,0:T(8,128)(2,1)}, bf16[4,192,512]{2,1,0:T(8,128)(2,1)}) custom-call(s32[6]{0:T(128)} %stack.42.scal, s32[1,192]{1,0:T(1,128)} %bitcast.56, bf16[4,6,1024,256]{3,2,1,0:T(8,128)(2,1)} %get-tuple-element.27.p_ref, ...), custom_call_target="tpu_custom_call" | custom-call | tf_op jit(solution)/shard_map/attention_grads/pallas_call | solution.py:290
  150.8 1.9 collective-permute-start.16
  153.2 2.7 %collective-permute-start.18 = (bf16[256,512]{1,0:T(8,128)(2,1)S(1)}, bf16[256,512]{1,0:T(8,128)(2,1)S(1)}, u32[]{:S(2)}, u32[]{:S(2)}) collective-permute-start(bf16[256,512]{1,0:T(8,128)(2,1)S(1)} %get-tuple-element.47), channel_id=1, source_target_pairs={{0,24},{8,0},{16,8},{24,16},{1,25},{9,1},{17,9},{25,17},{2,26},{10... | collective-permute-start | bytes 786440 | tf_op jit(solution)/shard_map/ppermute | solution.py:369
  156.1 5.5 %collective-permute-done.16 = bf16[256,512]{1,0:T(8,128)(2,1)S(1)} collective-permute-done((bf16[256,512]{1,0:T(8,128)(2,1)S(1)}, bf16[256,512]{1,0:T(8,128)(2,1)S(1)}, u32[]{:S(2)}, u32[]{:S(2)}) %collective-permute-start.16) | collective-permute-done | bytes 262176 | tf_op jit(solution)/shard_map/ppermute | solution.py:369
  161.6 4.6 %collective-permute-done.17 = bf16[256,512]{1,0:T(8,128)(2,1)S(1)} collective-permute-done((bf16[256,512]{1,0:T(8,128)(2,1)S(1)}, bf16[256,512]{1,0:T(8,128)(2,1)S(1)}, u32[]{:S(2)}, u32[]{:S(2)}) %collective-permute-start.17) | collective-permute-done | bytes 262176 | tf_op jit(solution)/shard_map/ppermute | solution.py:369
  166.2 2.3 %collective-permute-start.10 = (bf16[192,512]{1,0:T(8,128)(2,1)S(1)}, bf16[192,512]{1,0:T(8,128)(2,1)S(1)}, u32[]{:S(2)}, u32[]{:S(2)}) collective-permute-start(bf16[192,512]{1,0:T(8,128)(2,1)S(1)} %get-tuple-element.52), channel_id=1, source_target_pairs={{2,0},{3,1},{4,2},{5,3},{6,4},{7,5},{10,8},{11,9},{12,10},{13,11},... | collective-permute-start | bytes 589832 | tf_op jit(solution)/shard_map/ppermute | solution.py:328
  169.4 2.8 %collective-permute-start.19 = (bf16[256,512]{1,0:T(8,128)(2,1)S(1)}, bf16[256,512]{1,0:T(8,128)(2,1)S(1)}, u32[]{:S(2)}, u32[]{:S(2)}) collective-permute-start(bf16[256,512]{1,0:T(8,128)(2,1)S(1)} %fusion.3), channel_id=1, source_target_pairs={{0,0},{1,1},{2,32},{3,33},{4,64},{5,65},{6,96},{7,97},{32,2},{33,3... | collective-permute-start | bytes 786440 | tf_op jit(solution)/shard_map/ppermute | solution.py:376
  172.2 5.3 %collective-permute-start.20 = (bf16[256,512]{1,0:T(8,128)(2,1)S(1)}, bf16[256,512]{1,0:T(8,128)(2,1)S(1)}, u32[]{:S(2)}, u32[]{:S(2)}) collective-permute-start(bf16[256,512]{1,0:T(8,128)(2,1)S(1)} %fusion.3), channel_id=1, source_target_pairs={{0,32},{1,33},{2,64},{3,65},{4,96},{5,97},{6,0},{7,1},{32,34},{33,... | collective-permute-start | bytes 786440 | tf_op jit(solution)/shard_map/ppermute | solution.py:376
  177.5 2.8 %collective-permute-start.21 = (bf16[256,512]{1,0:T(8,128)(2,1)S(1)}, bf16[256,512]{1,0:T(8,128)(2,1)S(1)}, u32[]{:S(2)}, u32[]{:S(2)}) collective-permute-start(bf16[256,512]{1,0:T(8,128)(2,1)S(1)} %fusion.3), channel_id=1, source_target_pairs={{0,64},{1,65},{2,96},{3,97},{4,0},{5,1},{6,32},{7,33},{32,66},{33,... | collective-permute-start | bytes 786440 | tf_op jit(solution)/shard_map/ppermute | solution.py:376
  180.2 1.3 collective-permute-start.9
  182.5 7.2 %hidden_grad.1 = bf16[1,256,8192]{2,1,0:T(8,128)(2,1)} custom-call(bf16[256,512]{1,0:T(8,128)(2,1)} %convolution_convert_fusion.1.gv_ref, bf16[8192,512]{1,0:T(8,128)(2,1)} %all-gather.4.cloned.1.call-done.w_ref), custom_call_target="tpu_custom_call" | custom-call | tf_op jit(solution)/shard_map/hidden_grad/pallas_call | solution.py:173
  189.8 9.1 %collective-permute-done.9 = bf16[192,512]{1,0:T(8,128)(2,1)S(1)} collective-permute-done((bf16[192,512]{1,0:T(8,128)(2,1)S(1)}, bf16[192,512]{1,0:T(8,128)(2,1)S(1)}, u32[]{:S(2)}, u32[]{:S(2)}) %collective-permute-start.9) | collective-permute-done | bytes 196640 | tf_op jit(solution)/shard_map/ppermute | solution.py:328
  198.8 1.0 fusion
  (62 shorter events, 10.3 us)
Async XLA Ops:
  7.2 57.6 %all-gather.4.cloned.1.call-start = ((), (), s32[]{:S(2)}) async-start(), calls=%async_computation.1 | async-start | bytes 8650752 | tf_op jit(solution)/shard_map/all_gather | solution.py:348
  8.8 13.2 %copy-start.7 = (s32[192]{0:T(256)}, s32[192]{0:T(256)S(1)}, u32[]{:S(2)}) copy-start(s32[192]{0:T(256)S(1)} %dynamic_slice.3) | copy-start | bytes 2308
  9.0 13.0 %collective-permute-start = (bf16[192,512]{1,0:T(8,128)(2,1)S(1)}, bf16[192,512]{1,0:T(8,128)(2,1)S(1)}, u32[]{:S(2)}, u32[]{:S(2)}) collective-permute-start(bf16[192,512]{1,0:T(8,128)(2,1)S(1)} %convolution_convert_fusion.2), channel_id=1, source_target_pairs={{0,2},{1,3},{2,4},{3,5},{4,6},{5,7},{8,10},{9,11},{10,12},{11,13},... | collective-permute-start | bytes 589832 | tf_op jit(solution)/shard_map/ppermute | solution.py:317
  12.9 9.1 %collective-permute-start.1 = (bf16[192,512]{1,0:T(8,128)(2,1)S(1)}, bf16[192,512]{1,0:T(8,128)(2,1)S(1)}, u32[]{:S(2)}, u32[]{:S(2)}) collective-permute-start(bf16[192,512]{1,0:T(8,128)(2,1)S(1)} %convolution_convert_fusion.2), channel_id=1, source_target_pairs={{0,4},{1,5},{2,6},{3,7},{8,12},{9,13},{10,14},{11,15},{16,20},{17,... | collective-permute-start | bytes 589832 | tf_op jit(solution)/shard_map/ppermute | solution.py:317
  15.2 6.8 %collective-permute-start.2 = (bf16[192,512]{1,0:T(8,128)(2,1)S(1)}, bf16[192,512]{1,0:T(8,128)(2,1)S(1)}, u32[]{:S(2)}, u32[]{:S(2)}) collective-permute-start(bf16[192,512]{1,0:T(8,128)(2,1)S(1)} %convolution_convert_fusion.2), channel_id=1, source_target_pairs={{0,6},{1,7},{8,14},{9,15},{16,22},{17,23},{24,30},{25,31},{32,38},... | collective-permute-start | bytes 589832 | tf_op jit(solution)/shard_map/ppermute | solution.py:317
  23.0 48.4 %collective-permute-start.3 = (bf16[4,192,512]{2,1,0:T(8,128)(2,1)}, bf16[4,192,512]{2,1,0:T(8,128)(2,1)}, u32[]{:S(2)}, u32[]{:S(2)}) collective-permute-start(bf16[4,192,512]{2,1,0:T(8,128)(2,1)} %pad_maximum_fusion.ko_ref), channel_id=1, source_target_pairs={{0,1},{1,0},{2,3},{3,2},{4,5},{5,4},{6,7},{7,6},{8,9},{9,8},{10,11... | collective-permute-start | bytes 2359304 | tf_op jit(solution)/shard_map/ppermute | solution.py:321
  23.0 93.0 %all-to-all-start = ((bf16[4,192,2048]{2,1,0:T(8,128)(2,1)}), bf16[4,192,2048]{2,1,0:T(8,128)(2,1)S(1)}, u32[]{:S(2)}, u32[]{:S(2)}) async-start(bf16[4,192,2048]{2,1,0:T(8,128)(2,1)} %select_hidden.1.hid_ref), calls=%async_computation | async-start | bytes 6291456 | tf_op jit(solution)/shard_map/all_to_all | solution.py:353
  27.3 103.4 %all-gather.6.cloned.1.call-start = ((), (), s32[]{:S(2)}) async-start(), calls=%async_computation.2 | async-start | bytes 1769472 | tf_op jit(solution)/shard_map/all_gather | solution.py:361
  91.4 2.6 %collective-permute-start.4 = (bf16[4,192,512]{2,1,0:T(8,128)(2,1)}, bf16[4,192,512]{2,1,0:T(8,128)(2,1)S(1)}, u32[]{:S(2)}, u32[]{:S(2)}) collective-permute-start(bf16[4,192,512]{2,1,0:T(8,128)(2,1)} %get-tuple-element.34), channel_id=1, source_target_pairs={{0,1},{1,0},{2,3},{3,2},{4,5},{5,4},{6,7},{7,6},{8,9},{9,8},{10,11... | collective-permute-start | bytes 2359304 | tf_op jit(solution)/shard_map/ppermute | solution.py:326
  95.4 11.2 %collective-permute-start.5 = (bf16[192,512]{1,0:T(8,128)(2,1)S(1)}, bf16[192,512]{1,0:T(8,128)(2,1)S(1)}, u32[]{:S(2)}, u32[]{:S(2)}) collective-permute-start(bf16[192,512]{1,0:T(8,128)(2,1)S(1)} %get-tuple-element.56), channel_id=1, source_target_pairs={{4,0},{5,1},{6,2},{7,3},{12,8},{13,9},{14,10},{15,11},{20,16},{21,... | collective-permute-start | bytes 589832 | tf_op jit(solution)/shard_map/ppermute | solution.py:328
  96.7 13.5 %collective-permute-start.6 = (bf16[192,512]{1,0:T(8,128)(2,1)S(1)}, bf16[192,512]{1,0:T(8,128)(2,1)S(1)}, u32[]{:S(2)}, u32[]{:S(2)}) collective-permute-start(bf16[192,512]{1,0:T(8,128)(2,1)S(1)} %get-tuple-element.55), channel_id=1, source_target_pairs={{2,0},{3,1},{4,2},{5,3},{6,4},{7,5},{10,8},{11,9},{12,10},{13,11},... | collective-permute-start | bytes 589832 | tf_op jit(solution)/shard_map/ppermute | solution.py:328
  99.5 10.8 %collective-permute-start.7 = (bf16[192,512]{1,0:T(8,128)(2,1)S(1)}, bf16[192,512]{1,0:T(8,128)(2,1)S(1)}, u32[]{:S(2)}, u32[]{:S(2)}) collective-permute-start(bf16[192,512]{1,0:T(8,128)(2,1)S(1)} %get-tuple-element.54), channel_id=1, source_target_pairs={{6,0},{7,1},{14,8},{15,9},{22,16},{23,17},{30,24},{31,25},{38,32},... | collective-permute-start | bytes 589832 | tf_op jit(solution)/shard_map/ppermute | solution.py:328
  110.3 13.4 %copy-start.3 = (bf16[192,512]{1,0:T(8,128)(2,1)}, bf16[192,512]{1,0:T(8,128)(2,1)S(1)}, u32[]{:S(2)}) copy-start(bf16[192,512]{1,0:T(8,128)(2,1)S(1)} %add_convert_fusion.9.g0) | copy-start | bytes 589828
  110.4 8.2 %collective-permute-start.12 = (bf16[192,512]{1,0:T(8,128)(2,1)S(1)}, bf16[192,512]{1,0:T(8,128)(2,1)}, u32[]{:S(2)}, u32[]{:S(2)}) collective-permute-start(bf16[192,512]{1,0:T(8,128)(2,1)S(1)} %add_convert_fusion.9.g0), channel_id=1, source_target_pairs={{0,32},{32,64},{64,96},{96,0},{1,33},{33,65},{65,97},{97,1},{2,34}... | collective-permute-start | bytes 589832 | tf_op jit(solution)/shard_map/ppermute | solution.py:363
  111.9 11.8 %collective-permute-start.13 = (bf16[192,512]{1,0:T(8,128)(2,1)S(1)}, bf16[192,512]{1,0:T(8,128)(2,1)}, u32[]{:S(2)}, u32[]{:S(2)}) collective-permute-start(bf16[192,512]{1,0:T(8,128)(2,1)S(1)} %add_convert_fusion.9.g0), channel_id=1, source_target_pairs={{0,64},{32,96},{64,0},{96,32},{1,65},{33,97},{65,1},{97,33},{2,66}... | collective-permute-start | bytes 589832 | tf_op jit(solution)/shard_map/ppermute | solution.py:363
  114.6 9.1 %collective-permute-start.14 = (bf16[192,512]{1,0:T(8,128)(2,1)S(1)}, bf16[192,512]{1,0:T(8,128)(2,1)}, u32[]{:S(2)}, u32[]{:S(2)}) collective-permute-start(bf16[192,512]{1,0:T(8,128)(2,1)S(1)} %add_convert_fusion.9.g0), channel_id=1, source_target_pairs={{0,96},{32,0},{64,32},{96,64},{1,97},{33,1},{65,33},{97,65},{2,98}... | collective-permute-start | bytes 589832 | tf_op jit(solution)/shard_map/ppermute | solution.py:363
  130.7 19.9 %collective-permute-start.15 = (bf16[4,256,512]{2,1,0:T(8,128)(2,1)}, bf16[4,256,512]{2,1,0:T(8,128)(2,1)S(1)}, u32[]{:S(2)}, u32[]{:S(2)}) collective-permute-start(bf16[4,256,512]{2,1,0:T(8,128)(2,1)} %get-tuple-element.43), channel_id=1, source_target_pairs={{0,1},{1,0},{2,3},{3,2},{4,5},{5,4},{6,7},{7,6},{8,9},{9,8},{10,11... | collective-permute-start | bytes 3145736 | tf_op jit(solution)/shard_map/ppermute | solution.py:365
  130.7 19.8 %copy-start.5 = (bf16[4,256,512]{2,1,0:T(8,128)(2,1)S(1)}, bf16[4,256,512]{2,1,0:T(8,128)(2,1)}, u32[]{:S(2)}) copy-start(bf16[4,256,512]{2,1,0:T(8,128)(2,1)} %get-tuple-element.42) | copy-start | bytes 3145732
  150.0 5.9 %collective-permute-start.8 = (bf16[4,192,512]{2,1,0:T(8,128)(2,1)}, bf16[4,192,512]{2,1,0:T(8,128)(2,1)S(1)}, u32[]{:S(2)}, u32[]{:S(2)}) collective-permute-start(bf16[4,192,512]{2,1,0:T(8,128)(2,1)} %get-tuple-element.41), channel_id=1, source_target_pairs={{0,1},{1,0},{2,3},{3,2},{4,5},{5,4},{6,7},{7,6},{8,9},{9,8},{10,11... | collective-permute-start | bytes 2359304 | tf_op jit(solution)/shard_map/ppermute | solution.py:326
  150.7 30.8 %copy-start.4 = (bf16[192,512]{1,0:T(8,128)(2,1)S(1)}, bf16[192,512]{1,0:T(8,128)(2,1)}, u32[]{:S(2)}) copy-start(bf16[192,512]{1,0:T(8,128)(2,1)} %copy-done.3) | copy-start | bytes 589828
  150.8 30.8 %copy-start.8 = (s32[192]{0:T(256)S(1)}, s32[192]{0:T(256)}, u32[]{:S(2)}) copy-start(s32[192]{0:T(256)} %copy-done.7) | copy-start | bytes 2308
  150.8 10.8 %collective-permute-start.16 = (bf16[256,512]{1,0:T(8,128)(2,1)S(1)}, bf16[256,512]{1,0:T(8,128)(2,1)S(1)}, u32[]{:S(2)}, u32[]{:S(2)}) collective-permute-start(bf16[256,512]{1,0:T(8,128)(2,1)S(1)} %get-tuple-element.49), channel_id=1, source_target_pairs={{0,16},{8,24},{16,0},{24,8},{1,17},{9,25},{17,1},{25,9},{2,18},{10... | collective-permute-start | bytes 786440 | tf_op jit(solution)/shard_map/ppermute | solution.py:369
  152.6 13.6 %collective-permute-start.17 = (bf16[256,512]{1,0:T(8,128)(2,1)S(1)}, bf16[256,512]{1,0:T(8,128)(2,1)S(1)}, u32[]{:S(2)}, u32[]{:S(2)}) collective-permute-start(bf16[256,512]{1,0:T(8,128)(2,1)S(1)} %get-tuple-element.48), channel_id=1, source_target_pairs={{0,8},{8,16},{16,24},{24,0},{1,9},{9,17},{17,25},{25,1},{2,10},{10... | collective-permute-start | bytes 786440 | tf_op jit(solution)/shard_map/ppermute | solution.py:369
  153.2 13.0 %collective-permute-start.18 = (bf16[256,512]{1,0:T(8,128)(2,1)S(1)}, bf16[256,512]{1,0:T(8,128)(2,1)S(1)}, u32[]{:S(2)}, u32[]{:S(2)}) collective-permute-start(bf16[256,512]{1,0:T(8,128)(2,1)S(1)} %get-tuple-element.47), channel_id=1, source_target_pairs={{0,24},{8,0},{16,8},{24,16},{1,25},{9,1},{17,9},{25,17},{2,26},{10... | collective-permute-start | bytes 786440 | tf_op jit(solution)/shard_map/ppermute | solution.py:369
  166.2 14.0 %collective-permute-start.10 = (bf16[192,512]{1,0:T(8,128)(2,1)S(1)}, bf16[192,512]{1,0:T(8,128)(2,1)S(1)}, u32[]{:S(2)}, u32[]{:S(2)}) collective-permute-start(bf16[192,512]{1,0:T(8,128)(2,1)S(1)} %get-tuple-element.52), channel_id=1, source_target_pairs={{2,0},{3,1},{4,2},{5,3},{6,4},{7,5},{10,8},{11,9},{12,10},{13,11},... | collective-permute-start | bytes 589832 | tf_op jit(solution)/shard_map/ppermute | solution.py:328
  168.5 11.7 %collective-permute-start.11 = (bf16[192,512]{1,0:T(8,128)(2,1)S(1)}, bf16[192,512]{1,0:T(8,128)(2,1)S(1)}, u32[]{:S(2)}, u32[]{:S(2)}) collective-permute-start(bf16[192,512]{1,0:T(8,128)(2,1)S(1)} %get-tuple-element.51), channel_id=1, source_target_pairs={{6,0},{7,1},{14,8},{15,9},{22,16},{23,17},{30,24},{31,25},{38,32},... | collective-permute-start | bytes 589832 | tf_op jit(solution)/shard_map/ppermute | solution.py:328
  169.4 30.4 %collective-permute-start.19 = (bf16[256,512]{1,0:T(8,128)(2,1)S(1)}, bf16[256,512]{1,0:T(8,128)(2,1)S(1)}, u32[]{:S(2)}, u32[]{:S(2)}) collective-permute-start(bf16[256,512]{1,0:T(8,128)(2,1)S(1)} %fusion.3), channel_id=1, source_target_pairs={{0,0},{1,1},{2,32},{3,33},{4,64},{5,65},{6,96},{7,97},{32,2},{33,3... | collective-permute-start | bytes 786440 | tf_op jit(solution)/shard_map/ppermute | solution.py:376
  172.2 27.7 %collective-permute-start.20 = (bf16[256,512]{1,0:T(8,128)(2,1)S(1)}, bf16[256,512]{1,0:T(8,128)(2,1)S(1)}, u32[]{:S(2)}, u32[]{:S(2)}) collective-permute-start(bf16[256,512]{1,0:T(8,128)(2,1)S(1)} %fusion.3), channel_id=1, source_target_pairs={{0,32},{1,33},{2,64},{3,65},{4,96},{5,97},{6,0},{7,1},{32,34},{33,... | collective-permute-start | bytes 786440 | tf_op jit(solution)/shard_map/ppermute | solution.py:376
  177.5 22.4 %collective-permute-start.21 = (bf16[256,512]{1,0:T(8,128)(2,1)S(1)}, bf16[256,512]{1,0:T(8,128)(2,1)S(1)}, u32[]{:S(2)}, u32[]{:S(2)}) collective-permute-start(bf16[256,512]{1,0:T(8,128)(2,1)S(1)} %fusion.3), channel_id=1, source_target_pairs={{0,64},{1,65},{2,96},{3,97},{4,0},{5,1},{6,32},{7,33},{32,66},{33,... | collective-permute-start | bytes 786440 | tf_op jit(solution)/shard_map/ppermute | solution.py:376
  180.2 19.6 %collective-permute-start.22 = (bf16[256,512]{1,0:T(8,128)(2,1)S(1)}, bf16[256,512]{1,0:T(8,128)(2,1)S(1)}, u32[]{:S(2)}, u32[]{:S(2)}) collective-permute-start(bf16[256,512]{1,0:T(8,128)(2,1)S(1)} %fusion.3), channel_id=1, source_target_pairs={{0,96},{1,97},{2,0},{3,1},{4,32},{5,33},{6,64},{7,65},{32,98},{33,... | collective-permute-start | bytes 786440 | tf_op jit(solution)/shard_map/ppermute | solution.py:376
  180.2 18.6 %collective-permute-start.9 = (bf16[192,512]{1,0:T(8,128)(2,1)S(1)}, bf16[192,512]{1,0:T(8,128)(2,1)S(1)}, u32[]{:S(2)}, u32[]{:S(2)}) collective-permute-start(bf16[192,512]{1,0:T(8,128)(2,1)S(1)} %get-tuple-element.53), channel_id=1, source_target_pairs={{4,0},{5,1},{6,2},{7,3},{12,8},{13,9},{14,10},{15,11},{20,16},{21,... | collective-permute-start | bytes 589832 | tf_op jit(solution)/shard_map/ppermute | solution.py:328
  182.5 18.2 %copy-start.1 = (bf16[1,256,512]{2,1,0:T(8,128)(2,1)S(1)}, bf16[1,256,512]{2,1,0:T(8,128)(2,1)}, u32[]{:S(2)}) copy-start(bf16[1,256,512]{2,1,0:T(8,128)(2,1)} %param.8) | copy-start | bytes 786436
  (3 other events, 15.2 us)
Sparse Core Ops, SparseCore 0:
  10.3 54.5 all-gather.3
  71.6 22.6 all-gather.5
